TPU v7x, 128 devices: a whole 4x4x4 slice. The times are simulated.
128 devices in a mesh: wide: 16 (over z_hi, x, core), narrow: 8 (over z_lo, y).
Axes of the slice: x: 4, y: 4, z: 4 (z_hi: 2, z_lo: 2; z = z_hi * 2 + z_lo), core: 2. Of those that a mesh axis runs over, the one named last changes fastest.
Arguments:
- tokens: bfloat16 [12288, 1024], P(('wide', 'narrow')), may hold values from -6 to 6
- cotangent: bfloat16 [12288, 1024], P(('wide', 'narrow')), may hold values from -6 to 6
- segments: int32 [16, 768], P('wide'), may hold values from 0 to 3, never falling along the last dimension, each value on 1 to 384 neighbouring positions
- w_query: bfloat16 [1024, 1024], P(None, 'narrow'), may hold values from -0.1875 to 0.1875
- w_key: bfloat16 [1024, 1024], P(None, 'narrow'), may hold values from -0.1875 to 0.1875
- w_value: bfloat16 [1024, 1024], P(None, 'narrow'), may hold values from -0.1875 to 0.1875
- w_out: bfloat16 [1024, 1024], P('narrow'), may hold values from -1.5 to 1.5
- w_gate: bfloat16 [1024, 4096], P(None, 'narrow'), may hold values from -0.1875 to 0.1875
- w_up: bfloat16 [1024, 4096], P(None, 'narrow'), may hold values from -0.1875 to 0.1875
- w_down: bfloat16 [4096, 1024], P('narrow'), may hold values from -0.09375 to 0.09375
- gain_one: float32 [1024], replicated, may hold values from 0.25 to 1.75
- bias_one: float32 [1024], replicated, may hold values from -2.5 to 2.5
- gain_two: float32 [1024], replicated, may hold values from 0.25 to 1.75
- bias_two: float32 [1024], replicated, may hold values from -2.5 to 2.5
Outputs:
- layer_out: float32 [12288, 1024], P(('wide', 'narrow'))
- input_grad: float32 [12288, 1024], P(('wide', 'narrow'))
- grad_query: float32 [1024, 1024], P(None, 'narrow')
- grad_key: float32 [1024, 1024], P(None, 'narrow')
- grad_value: float32 [1024, 1024], P(None, 'narrow')
- grad_out: float32 [1024, 1024], P('narrow')
- grad_gate: float32 [1024, 4096], P(None, 'narrow')
- grad_up: float32 [1024, 4096], P(None, 'narrow')
- grad_down: float32 [4096, 1024], P('narrow')
- grad_gain_one: float32 [1024], replicated
- grad_bias_one: float32 [1024], replicated
- grad_gain_two: float32 [1024], replicated
- grad_bias_two: float32 [1024], replicated
Inputs may be any that keep to these rules, and one draw needn't show every extreme that they name: `segments`: within each row of 768 tokens segment numbers never fall; each segment holds 1 to 384 tokens and one holds exactly 384.
All inputs are finite; a program needn't handle non-finite values.
Results may differ from a plain program's by a relative error of at most 0.03.
Values may be sent and summed in bfloat16 or wider, within the bound.
No kernel may reach another device: no remote copies, remote signals or barrier semaphores. Data moves between devices by JAX's collectives and lax.ppermute only.
A program may use at most 128 MiB of HBM per device.

v0:
```python
import math
import jax
import jax.numpy as jnp
from jax import lax
from jax.sharding import PartitionSpec as P

HD = 64
EPS = 1e-05
MASKED = -1e30


def normalize(values, gain_vec, bias_vec):
    centred = values - jnp.mean(values, axis=-1, keepdims=True)
    inverse = lax.rsqrt(jnp.mean(centred * centred, axis=-1, keepdims=True) + EPS)
    scaled = centred * inverse
    return (scaled * gain_vec + bias_vec, scaled, inverse)


def normalize_back(grad_in, scaled, inverse, gain_vec):
    along = grad_in * gain_vec
    return inverse * (
        along
        - jnp.mean(along, axis=-1, keepdims=True)
        - scaled * jnp.mean(along * scaled, axis=-1, keepdims=True)
    )


def contract_last(left_side, right_side):
    return lax.dot_general(
        left_side, right_side, (((1,), (1,)), ((), ())), preferred_element_type=jnp.float32
    )


def contract_first(left_side, right_side):
    return lax.dot_general(
        left_side, right_side, (((0,), (0,)), ((), ())), preferred_element_type=jnp.float32
    )


def rotary_tables(seg_rows):
    length = seg_rows.shape[-1]
    column = lax.broadcasted_iota(jnp.int32, (length, length), 1)
    row_index = lax.broadcasted_iota(jnp.int32, (length,), 0)
    same_segment = seg_rows[..., :, None] == seg_rows[..., None, :]
    first_index = jnp.min(jnp.where(same_segment, column, length), axis=-1)
    position = (row_index - first_index).astype(jnp.float32)
    half_width = HD // 2
    inverse = 10000.0 ** (-(2.0 * jnp.arange(half_width).astype(jnp.float32) / HD))
    angles = position[..., None] * inverse
    return (jnp.cos(angles), jnp.sin(angles), same_segment)


def rotate(values, cosine_table, sine_table):
    half_width = values.shape[-1] // 2
    first_half = values[..., :half_width]
    second_half = values[..., half_width:]
    cosine = cosine_table[..., None, :]
    sine_part = sine_table[..., None, :]
    return jnp.concatenate(
        [
            first_half * cosine - second_half * sine_part,
            second_half * cosine + first_half * sine_part,
        ],
        axis=-1,
    )


def unrotate(values, cosine_table, sine_table):
    half_width = values.shape[-1] // 2
    first_half = values[..., :half_width]
    second_half = values[..., half_width:]
    cosine = cosine_table[..., None, :]
    sine_part = sine_table[..., None, :]
    return jnp.concatenate(
        [
            first_half * cosine + second_half * sine_part,
            second_half * cosine - first_half * sine_part,
        ],
        axis=-1,
    )


def project_heads(normed_one, w_query, w_key, w_value, cosine_table, sine_table):
    row_count, length = (cosine_table.shape[0], cosine_table.shape[1])
    head_shape = (row_count, length, w_query.shape[1] // HD, HD)
    queries = rotate(
        jnp.dot(normed_one, w_query, preferred_element_type=jnp.float32).reshape(head_shape),
        cosine_table,
        sine_table,
    ).astype(jnp.bfloat16)
    key_rows = rotate(
        jnp.dot(normed_one, w_key, preferred_element_type=jnp.float32).reshape(head_shape),
        cosine_table,
        sine_table,
    ).astype(jnp.bfloat16)
    value_rows = (
        jnp.dot(normed_one, w_value, preferred_element_type=jnp.float32)
        .astype(jnp.bfloat16)
        .reshape(head_shape)
    )
    return (queries, key_rows, value_rows)


def attention_forward(normed_one, w_query, w_key, w_value, cosine_table, sine_table, same_segment):
    queries, key_rows, value_rows = project_heads(
        normed_one, w_query, w_key, w_value, cosine_table, sine_table
    )
    score_scale = 1.0 / math.sqrt(HD)

    def one_row(row_items):
        query_row, key_row, value_row, mask_row = row_items
        scores = (
            jnp.einsum("qhd,khd->hqk", query_row, key_row, preferred_element_type=jnp.float32)
            * score_scale
        )
        scores = jnp.where(mask_row[None], scores, MASKED)
        row_peak = jnp.max(scores, axis=-1, keepdims=True)
        exponent = jnp.exp(scores - row_peak)
        row_total = jnp.sum(exponent, axis=-1, keepdims=True)
        probs_low = (exponent / row_total).astype(jnp.bfloat16)
        output = jnp.einsum(
            "hqk,khd->qhd", probs_low, value_row, preferred_element_type=jnp.float32
        ).astype(jnp.bfloat16)
        return (output, row_peak + jnp.log(row_total))

    attended, log_total = lax.map(one_row, (queries, key_rows, value_rows, same_segment))
    return (attended.reshape(normed_one.shape[0], -1), log_total)


def attention_grads(
    normed_one,
    attended,
    log_total,
    branch_grad,
    w_query,
    w_key,
    w_value,
    w_out,
    cosine_table,
    sine_table,
    same_segment,
):
    queries, key_rows, value_rows = project_heads(
        normed_one, w_query, w_key, w_value, cosine_table, sine_table
    )
    score_scale = 1.0 / math.sqrt(HD)
    grad_out = contract_first(attended, branch_grad)
    attended_grad = contract_last(branch_grad, w_out).astype(jnp.bfloat16).reshape(queries.shape)

    def one_row(row_items):
        query_row, key_row, value_row, mask_row, total_row, grad_row = row_items
        scores = (
            jnp.einsum("qhd,khd->hqk", query_row, key_row, preferred_element_type=jnp.float32)
            * score_scale
        )
        scores = jnp.where(mask_row[None], scores, MASKED)
        probs = jnp.exp(scores - total_row)
        probs_low = probs.astype(jnp.bfloat16)
        prob_grad = jnp.einsum(
            "qhd,khd->hqk", grad_row, value_row, preferred_element_type=jnp.float32
        )
        score_grad = (
            probs * (prob_grad - jnp.sum(probs * prob_grad, axis=-1, keepdims=True))
        ).astype(jnp.bfloat16)
        query_grad = score_scale * jnp.einsum(
            "hqk,khd->qhd", score_grad, key_row, preferred_element_type=jnp.float32
        )
        key_grad = score_scale * jnp.einsum(
            "hqk,qhd->khd", score_grad, query_row, preferred_element_type=jnp.float32
        )
        value_grad = jnp.einsum(
            "hqk,qhd->khd", probs_low, grad_row, preferred_element_type=jnp.float32
        ).astype(jnp.bfloat16)
        return (query_grad, key_grad, value_grad)

    query_grad, key_grad, value_grad = lax.map(
        one_row, (queries, key_rows, value_rows, same_segment, log_total, attended_grad)
    )
    token_count = normed_one.shape[0]
    query_grad = (
        unrotate(query_grad, cosine_table, sine_table).astype(jnp.bfloat16).reshape(token_count, -1)
    )
    key_grad = (
        unrotate(key_grad, cosine_table, sine_table).astype(jnp.bfloat16).reshape(token_count, -1)
    )
    value_grad = value_grad.reshape(token_count, -1)
    grad_query = contract_first(normed_one, query_grad)
    grad_key = contract_first(normed_one, key_grad)
    grad_value = contract_first(normed_one, value_grad)
    partial_sum = (
        contract_last(query_grad, w_query)
        + contract_last(key_grad, w_key)
        + contract_last(value_grad, w_value)
    )
    return (partial_sum, grad_query, grad_key, grad_value, grad_out)


def swiglu(normed_two, w_gate, w_up):
    gate_pre = jnp.dot(normed_two, w_gate, preferred_element_type=jnp.float32)
    up_pre = jnp.dot(normed_two, w_up, preferred_element_type=jnp.float32)
    sigmoid_gate = jax.nn.sigmoid(gate_pre)
    active = gate_pre * sigmoid_gate
    hidden = (active * up_pre).astype(jnp.bfloat16)
    return (hidden, gate_pre, up_pre, sigmoid_gate, active)


def swiglu_grads(normed_two, out_grad, w_gate, w_up, w_down):
    hidden, gate_pre, up_pre, sigmoid_gate, active = swiglu(normed_two, w_gate, w_up)
    hidden_grad = contract_last(out_grad, w_down)
    grad_down = contract_first(hidden, out_grad)
    gate_grad = (
        hidden_grad * up_pre * sigmoid_gate * (1.0 + gate_pre * (1.0 - sigmoid_gate))
    ).astype(jnp.bfloat16)
    up_grad = (hidden_grad * active).astype(jnp.bfloat16)
    grad_gate = contract_first(normed_two, gate_grad)
    grad_up = contract_first(normed_two, up_grad)
    partial_sum = contract_last(gate_grad, w_gate) + contract_last(up_grad, w_up)
    return (partial_sum, grad_gate, grad_up, grad_down)


def per_device(
    tokens,
    cotangent,
    segments,
    w_query,
    w_key,
    w_value,
    w_out,
    w_gate,
    w_up,
    w_down,
    gain_one,
    bias_one,
    gain_two,
    bias_two,
):
    shard_rows = tokens.shape[0]
    narrow_index = lax.axis_index("narrow")
    cosine_table, sine_table, same_segment = rotary_tables(segments)
    gathered, cot_whole = (
        lax.all_gather(tokens, "narrow", axis=0, tiled=True),
        lax.all_gather(cotangent, "narrow", axis=0, tiled=True),
    )
    inputs = gathered.astype(jnp.float32)
    normed_float, scaled_one, inverse_one = normalize(inputs, gain_one, bias_one)
    normed_one = normed_float.astype(jnp.bfloat16)
    attended, log_total = attention_forward(
        normed_one, w_query, w_key, w_value, cosine_table, sine_table, same_segment
    )
    middle = inputs + lax.psum(
        jnp.dot(attended, w_out, preferred_element_type=jnp.float32).astype(jnp.bfloat16), "narrow"
    ).astype(jnp.float32)
    normed_float_two, scaled_two, inverse_two = normalize(middle, gain_two, bias_two)
    normed_two = normed_float_two.astype(jnp.bfloat16)
    hidden = swiglu(normed_two, w_gate, w_up)[0]
    result_whole = middle + lax.psum(
        jnp.dot(hidden, w_down, preferred_element_type=jnp.float32).astype(jnp.bfloat16), "narrow"
    ).astype(jnp.float32)
    layer_out = lax.dynamic_slice_in_dim(result_whole, narrow_index * shard_rows, shard_rows, 0)
    partial_two, grad_gate, grad_up, grad_down = swiglu_grads(
        normed_two, cot_whole, w_gate, w_up, w_down
    )
    normed_two_grad = lax.psum(partial_two.astype(jnp.bfloat16), "narrow").astype(jnp.float32)
    middle_grad = cot_whole.astype(jnp.float32) + normalize_back(
        normed_two_grad, scaled_two, inverse_two, gain_two
    )
    own_two_grad = lax.dynamic_slice_in_dim(
        normed_two_grad, narrow_index * shard_rows, shard_rows, 0
    )
    own_scaled_two = lax.dynamic_slice_in_dim(scaled_two, narrow_index * shard_rows, shard_rows, 0)
    branch_grad = middle_grad.astype(jnp.bfloat16)
    partial_one, grad_query, grad_key, grad_value, grad_out = attention_grads(
        normed_one,
        attended,
        log_total,
        branch_grad,
        w_query,
        w_key,
        w_value,
        w_out,
        cosine_table,
        sine_table,
        same_segment,
    )
    normed_one_grad = lax.psum(partial_one.astype(jnp.bfloat16), "narrow").astype(jnp.float32)
    input_whole = middle_grad + normalize_back(normed_one_grad, scaled_one, inverse_one, gain_one)
    input_grad = lax.dynamic_slice_in_dim(input_whole, narrow_index * shard_rows, shard_rows, 0)
    own_one_grad = lax.dynamic_slice_in_dim(
        normed_one_grad, narrow_index * shard_rows, shard_rows, 0
    )
    own_scaled_one = lax.dynamic_slice_in_dim(scaled_one, narrow_index * shard_rows, shard_rows, 0)
    matrices = (
        lax.psum(grad_query.astype(jnp.bfloat16), "wide").astype(jnp.float32),
        lax.psum(grad_key.astype(jnp.bfloat16), "wide").astype(jnp.float32),
        lax.psum(grad_value.astype(jnp.bfloat16), "wide").astype(jnp.float32),
        lax.psum(grad_out.astype(jnp.bfloat16), "wide").astype(jnp.float32),
        lax.psum(grad_gate.astype(jnp.bfloat16), "wide").astype(jnp.float32),
        lax.psum(grad_up.astype(jnp.bfloat16), "wide").astype(jnp.float32),
        lax.psum(grad_down.astype(jnp.bfloat16), "wide").astype(jnp.float32),
    )
    norm_grads = lax.psum(
        (
            jnp.sum(own_one_grad * own_scaled_one, axis=0),
            jnp.sum(own_one_grad, axis=0),
            jnp.sum(own_two_grad * own_scaled_two, axis=0),
            jnp.sum(own_two_grad, axis=0),
        ),
        ("wide", "narrow"),
    )
    return (
        layer_out,
        input_grad,
        matrices[0],
        matrices[1],
        matrices[2],
        matrices[3],
        matrices[4],
        matrices[5],
        matrices[6],
        norm_grads[0],
        norm_grads[1],
        norm_grads[2],
        norm_grads[3],
    )


def solution(mesh):
    placed = (
        P(("wide", "narrow"), None),
        P(("wide", "narrow"), None),
        P("wide", None),
        P(None, "narrow"),
        P(None, "narrow"),
        P(None, "narrow"),
        P("narrow", None),
        P(None, "narrow"),
        P(None, "narrow"),
        P("narrow", None),
        P(),
        P(),
        P(),
        P(),
    )
    return jax.shard_map(
        per_device,
        mesh=mesh,
        in_specs=placed,
        out_specs=(
            P(("wide", "narrow"), None),
            P(("wide", "narrow"), None),
            P(None, "narrow"),
            P(None, "narrow"),
            P(None, "narrow"),
            P("narrow", None),
            P(None, "narrow"),
            P(None, "narrow"),
            P("narrow", None),
            P(),
            P(),
            P(),
            P(),
        ),
        check_vma=False,
    )
```

profile of v0, /device:TPU:0, one launch (start us, length us, event | category | flops | bytes accessed | tf_op | source)
XLA Modules:
  0.0 550.6 jit_solution(14009956408082012891)
XLA Ops:
  10.9 41.9 %all-gather.3.cloned.1.call-done = bf16[768,1024]{1,0:T(8,128)(2,1)} async-done(((bf16[96,1024]{1,0:T(8,128)(2,1)}), bf16[768,1024]{1,0:T(8,128)(2,1)}) %all-gather.3.cloned.1.call-update) | async-done | bytes 1572880 | tf_op jit(solution)/shard_map/all_gather | solution.py:241
  52.8 1.8 convert_reduce_fusion
  54.6 2.0 fusion.4
  63.5 1.7 convolution_convert_fusion.1
  66.2 77.9 %all-reduce.8.cloned.1.call-done = bf16[768,1024]{1,0:T(8,128)(2,1)} async-done(((bf16[768,1024]{1,0:T(8,128)(2,1)}), bf16[768,1024]{1,0:T(8,128)(2,1)}) %all-reduce.8.cloned.1.call-update) | async-done | bytes 1572880 | tf_op jit(solution)/shard_map/psum | solution.py:250
  144.1 2.0 fusion.28
  146.9 3.6 add_convert_fusion.2
  150.4 2.1 fusion.32
  152.6 2.1 fusion.33
  154.7 31.3 %all-gather.5.cloned.1.call-done = bf16[768,1024]{1,0:T(8,128)(2,1)} async-done(((bf16[96,1024]{1,0:T(8,128)(2,1)}), bf16[768,1024]{1,0:T(8,128)(2,1)}) %all-gather.5.cloned.1.call-update) | async-done | bytes 1572880 | tf_op jit(solution)/shard_map/all_gather | solution.py:242
  185.9 5.0 multiply_convert_fusion.1
  192.7 2.2 add_convert_fusion.1
  195.2 3.3 convolution_convert_fusion
  198.4 75.3 %all-reduce.10.cloned.1.call-done = bf16[768,1024]{1,0:T(8,128)(2,1)} async-done(((bf16[768,1024]{1,0:T(8,128)(2,1)}), bf16[768,1024]{1,0:T(8,128)(2,1)}) %all-reduce.10.cloned.1.call-update) | async-done | bytes 1572880 | tf_op jit(solution)/shard_map/psum | solution.py:263
  273.7 3.2 multiply_reduce_fusion.4
  277.5 2.6 multiply_add_fusion
  286.7 1.8 add_convert_fusion
  288.8 3.7 convolution_convert_fusion.3
  292.6 2.0 convolution_convert_fusion.4
  294.6 2.0 convolution_convert_fusion.2
  296.6 1.3 convolution_convert_fusion.6
  297.9 1.3 convolution_convert_fusion.7
  301.8 3.4 convert_element_type.182
  305.2 73.7 %all-reduce.14.cloned.1.call-done = (bf16[768,1024]{1,0:T(8,128)(2,1)}, bf16[768,1024]{1,0:T(8,128)(2,1)}) async-done(((bf16[768,1024]{1,0:T(8,128)(2,1)}, bf16[768,1024]{1,0:T(8,128)(2,1)}), (bf16[768,1024]{1,0:T(8,128)(2,1)}, bf16[768,1024]{1,0:T(8,128)(2,1)})) %all-reduce.14.cloned.1.call-update) | async-done | bytes 3145744 | tf_op jit(solution)/shard_map/psum | solution.py:256
  378.9 1.9 convert_element_type.192
  382.2 2.2 dynamic-slice_reduce_fusion
  384.4 65.4 %all-reduce = (f32[1024]{0:T(1024)}, f32[1024]{0:T(1024)}, f32[1024]{0:T(1024)}, f32[1024]{0:T(1024)}) all-reduce(f32[1024]{0:T(1024)S(1)} %get-tuple-element.113, f32[1024]{0:T(1024)S(1)} %get-tuple-element.114, f32[1024]{0:T(1024)S(1)} %get-tuple-element.55, ...), channel_id=1, replica_groups=mesh['wide'=16,'narrow'=8] {'wide','narrow'}, use_global_device_ids=true, to_apply=%region_24.25 | all-reduce | flops 4096 | bytes 32768 | tf_op jit(solution)/shard_map/psum | solution.py:301
  449.8 1.8 dynamic-slice_add_fusion.1
  451.6 82.6 %all-reduce.12.cloned.1.call-done = (bf16[1024,128]{1,0:T(8,128)(2,1)}, bf16[1024,128]{1,0:T(8,128)(2,1)}, bf16[1024,128]{1,0:T(8,128)(2,1)}, bf16[128,1024]{1,0...) async-done(((bf16[1024,128]{1,0:T(8,128)(2,1)}, bf16[1024,128]{1,0:T(8,128)(2,1)}, bf16[1024,128]{1,0:T(8,128)(2,1)}, ...) | async-done | bytes 4194320 | tf_op jit(solution)/shard_map/psum | solution.py:293
  534.2 3.0 convert_element_type.202
  537.2 1.6 convert_element_type.204
  538.8 1.6 convert_element_type.206
  (169 shorter events, 28.7 us)
Async XLA Ops:
  7.2 178.8 %copy-start = (bf16[512,1024]{1,0:T(8,128)(2,1)S(1)}, bf16[512,1024]{1,0:T(8,128)(2,1)}, u32[]{:S(2)}) copy-start(bf16[512,1024]{1,0:T(8,128)(2,1)} %param.23) | copy-start | bytes 3145732
  7.2 49.4 %copy-start.49 = (f32[1024]{0:T(1024)S(1)}, f32[1024]{0:T(1024)}, u32[]{:S(2)}) copy-start(f32[1024]{0:T(1024)} %param.24) | copy-start | bytes 12292
  7.2 49.4 %copy-start.50 = (f32[1024]{0:T(1024)S(1)}, f32[1024]{0:T(1024)}, u32[]{:S(2)}) copy-start(f32[1024]{0:T(1024)} %param.25) | copy-start | bytes 12292
  7.2 45.6 %all-gather.3.cloned.1.call-start = ((), (), s32[]{:S(2)}) async-start(), calls=%async_computation | async-start | bytes 1769472 | tf_op jit(solution)/shard_map/all_gather | solution.py:241
  8.0 136.2 %all-reduce.8.cloned.1.call-start = ((), (), s32[]{:S(2)}) async-start(), calls=%async_computation.1 | async-start | bytes 3145728 | tf_op jit(solution)/shard_map/psum | solution.py:250
  9.7 49.7 %copy-start.26 = (f32[768,32]{0,1:T(8,128)}, f32[768,32]{0,1:T(8,128)S(1)}, u32[]{:S(2)}) copy-start(f32[768,32]{0,1:T(8,128)S(1)} %get-tuple-element.107) | copy-start | bytes 294916
  10.9 46.4 %copy-start.22 = (bf16[1024,128]{1,0:T(8,128)(2,1)S(1)}, bf16[1024,128]{1,0:T(8,128)(2,1)}, u32[]{:S(2)}) copy-start(bf16[1024,128]{1,0:T(8,128)(2,1)} %param.17) | copy-start | bytes 786436
  52.8 3.9 copy-start.2
  54.6 3.4 copy-start.21
  65.2 120.7 %all-gather.5.cloned.1.call-start = ((), (), s32[]{:S(2)}) async-start(), calls=%async_computation.2 | async-start | bytes 1769472 | tf_op jit(solution)/shard_map/all_gather | solution.py:242
  66.0 80.9 %copy-start.48 = (f32[1024]{0:T(1024)S(1)}, f32[1024]{0:T(1024)}, u32[]{:S(2)}) copy-start(f32[1024]{0:T(1024)} %param.26) | copy-start | bytes 12292
  66.0 80.9 %copy-start.51 = (f32[1024]{0:T(1024)S(1)}, f32[1024]{0:T(1024)}, u32[]{:S(2)}) copy-start(f32[1024]{0:T(1024)} %param.27) | copy-start | bytes 12292
  66.0 207.7 %all-reduce.10.cloned.1.call-start = ((), (), s32[]{:S(2)}) async-start(), calls=%async_computation.3 | async-start | bytes 3145728 | tf_op jit(solution)/shard_map/psum | solution.py:263
  146.9 3.6 copy-start.15
  185.9 5.0 copy-start.16
  194.9 184.0 %all-reduce.14.cloned.1.call-start = ((), (), s32[]{:S(2)}) async-start(), calls=%async_computation.5 | async-start | bytes 6291456 | tf_op jit(solution)/shard_map/psum | solution.py:256
  273.7 3.3 copy-start.8
  273.7 3.8 copy-start.9
  273.7 7.0 %slice-start = ((s8[4718592]{0:T(1024)(128)(4,1)}), s8[4194304]{0:T(1024)(128)(4,1)S(1)}, s32[]{:S(2)}) async-start(s8[4718592]{0:T(1024)(128)(4,1)} %bitcast.74), calls=%async_computation.6 | async-start | bytes 8388608
  277.5 3.3 slice-start.1
  288.5 4.1 copy-start.29
  288.5 245.7 %all-reduce.12.cloned.1.call-start = ((), (), s32[]{:S(2)}) async-start(), calls=%async_computation.4 | async-start | bytes 8388608 | tf_op jit(solution)/shard_map/psum | solution.py:293
  288.8 3.7 copy-start.14
  296.6 4.0 copy-start.7
  296.6 4.0 copy-start.32
  534.2 3.0 copy-start.20
  534.2 4.6 copy-start.19
  537.2 3.2 copy-start.47
  537.2 4.0 copy-start.46
  538.8 3.2 copy-start.45
  538.8 4.1 copy-start.44
  538.8 4.9 copy-start.1
  (29 other events, 46.5 us)
Sparse Core Ops, SparseCore 0:
  9.7 43.0 all-gather.2
  65.4 78.7 all-reduce.7
  145.8 40.1 all-gather.4
  195.0 78.6 all-reduce.9
  288.6 90.2 all-reduce.13
  382.4 151.7 all-reduce.11
where the time goes:
time: 551 us
  waiting for transfers between devices  384 us (70%)
  blocking collectives  65.4 us (12%)
  other arithmetic  41.2 us (7%)
  matrix products  41 us (7%)
  between operations  14.8 us (3%)
    psum x1, waiting for transfers between devices, per_device(): lax.psum(grad_query.astype(jnp.bfloat16), 'wide').astype(jnp.float32)  82.6 us
    psum x1, waiting for transfers between devices, per_device(): lax.psum(jnp.dot(attended, w_out, preferred_element_type=jnp.float32).ast...  77.9 us
    psum x1, waiting for transfers between devices, per_device(): lax.psum(partial_two.astype(jnp.bfloat16), 'narrow').astype(jnp.float32)  75.3 us
    psum x1, waiting for transfers between devices, per_device(): lax.psum(jnp.dot(hidden, w_down, preferred_element_type=jnp.float32).asty...  73.7 us
    psum x1, blocking collectives, per_device(): lax.psum((jnp.sum(own_one_grad * own_scaled_one, axis=0), jnp.sum(own_one...  65.4 us
    all_gather x1, waiting for transfers between devices, per_device(): lax.all_gather(tokens, 'narrow', axis=0, tiled=True)  41.9 us
    all_gather x1, waiting for transfers between devices, per_device(): lax.all_gather(cotangent, 'narrow', axis=0, tiled=True)  31.3 us
    dot_general x7, matrix products, contract_first(): lax.dot_general(left_side, right_side, (((0,), (0,)), ((), ())), preferre...  12.8 us
  transfers between devices with their start and end apart: 6, of which 6 were waited for; matrix products, arithmetic and copies ran while one was open for 7% of the time, Pallas kernels for 0%

commit v1 on v0

--- a/solution.py
+++ b/solution.py
@@ -290,7 +290,9 @@
     )
     own_scaled_one = lax.dynamic_slice_in_dim(scaled_one, narrow_index * shard_rows, shard_rows, 0)
     matrices = (
-        lax.psum(grad_query.astype(jnp.bfloat16), "wide").astype(jnp.float32),
+        jnp.sum(jax.lax.all_gather(grad_query.astype(jnp.bfloat16), "wide"), axis=0).astype(
+            jnp.float32
+        ),
         lax.psum(grad_key.astype(jnp.bfloat16), "wide").astype(jnp.float32),
         lax.psum(grad_value.astype(jnp.bfloat16), "wide").astype(jnp.float32),
         lax.psum(grad_out.astype(jnp.bfloat16), "wide").astype(jnp.float32),

time: 551 us -> 605 us (1.098)
  waiting for transfers between devices: 384 us -> 430 us
    all_gather x0 -> x1, waiting for transfers between devices: none -> 48.3 us  [per_device(): jax.lax.all_gather(grad_query.astype(jnp.bfloat16), 'wide')]
  transfers between devices with their start and end apart: 6 -> 7, of which waited for: 6 -> 7; matrix products, arithmetic and copies ran while one was open for 7% -> 9% of each run, Pallas kernels for 0% -> 0%
where the time goes in v1:
time: 605 us; the launch traced here: 604 us
  waiting for transfers between devices  430 us (71%)
  blocking collectives  65.2 us (11%)
  other arithmetic  46.7 us (8%)
  matrix products  42.6 us (7%)
  between operations  14.8 us (2%)
    psum x1, waiting for transfers between devices, per_device(): lax.psum(grad_key.astype(jnp.bfloat16), 'wide').astype(jnp.float32)  81.8 us
    psum x1, waiting for transfers between devices, per_device(): lax.psum(jnp.dot(attended, w_out, preferred_element_type=jnp.float32).ast...  77.9 us
    psum x1, waiting for transfers between devices, per_device(): lax.psum(partial_two.astype(jnp.bfloat16), 'narrow').astype(jnp.float32)  75.3 us
    psum x1, waiting for transfers between devices, per_device(): lax.psum(jnp.dot(hidden, w_down, preferred_element_type=jnp.float32).asty...  72.6 us
    psum x1, blocking collectives, per_device(): lax.psum((jnp.sum(own_one_grad * own_scaled_one, axis=0), jnp.sum(own_one...  65.2 us
    all_gather x1, waiting for transfers between devices, per_device(): jax.lax.all_gather(grad_query.astype(jnp.bfloat16), 'wide')  48.3 us
    all_gather x1, waiting for transfers between devices, per_device(): lax.all_gather(tokens, 'narrow', axis=0, tiled=True)  41.2 us
    all_gather x1, waiting for transfers between devices, per_device(): lax.all_gather(cotangent, 'narrow', axis=0, tiled=True)  31.3 us
  transfers between devices with their start and end apart: 7, of which 7 were waited for; matrix products, arithmetic and copies ran while one was open for 9% of the time, Pallas kernels for 0%

profile of v1, /device:TPU:0, one launch (start us, length us, event | category | flops | bytes accessed | tf_op | source)
XLA Modules:
  0.0 603.5 jit_solution(15980570187241223353)
XLA Ops:
  11.5 41.2 %all-gather.5.cloned.1.call-done = bf16[768,1024]{1,0:T(8,128)(2,1)} async-done(((bf16[96,1024]{1,0:T(8,128)(2,1)}), bf16[768,1024]{1,0:T(8,128)(2,1)}) %all-gather.5.cloned.1.call-update) | async-done | bytes 1572880 | tf_op jit(solution)/shard_map/all_gather | solution.py:241
  52.8 1.8 convert_reduce_fusion
  54.6 2.0 fusion.4
  66.2 77.9 %all-reduce.8.cloned.1.call-done = bf16[768,1024]{1,0:T(8,128)(2,1)} async-done(((bf16[768,1024]{1,0:T(8,128)(2,1)}), bf16[768,1024]{1,0:T(8,128)(2,1)}) %all-reduce.8.cloned.1.call-update) | async-done | bytes 1572880 | tf_op jit(solution)/shard_map/psum | solution.py:250
  144.2 2.0 fusion.28
  147.0 3.5 add_convert_fusion.2
  150.5 2.1 fusion.33
  152.6 2.1 fusion.32
  154.7 31.3 %all-gather.7.cloned.1.call-done = bf16[768,1024]{1,0:T(8,128)(2,1)} async-done(((bf16[96,1024]{1,0:T(8,128)(2,1)}), bf16[768,1024]{1,0:T(8,128)(2,1)}) %all-gather.7.cloned.1.call-update) | async-done | bytes 1572880 | tf_op jit(solution)/shard_map/all_gather | solution.py:242
  186.0 5.0 multiply_convert_fusion.1
  192.8 2.2 add_convert_fusion.1
  195.3 3.3 convolution_convert_fusion
  198.5 75.3 %all-reduce.10.cloned.1.call-done = bf16[768,1024]{1,0:T(8,128)(2,1)} async-done(((bf16[768,1024]{1,0:T(8,128)(2,1)}), bf16[768,1024]{1,0:T(8,128)(2,1)}) %all-reduce.10.cloned.1.call-update) | async-done | bytes 1572880 | tf_op jit(solution)/shard_map/psum | solution.py:263
  273.9 3.2 multiply_reduce_fusion.4
  277.6 2.6 multiply_add_fusion
  288.7 3.8 convolution_convert_fusion.3
  292.5 2.0 convolution_convert_fusion.4
  294.6 2.0 convolution_convert_fusion.2
  300.7 2.7 convolution_convert_fusion.8
  303.5 1.8 convert_element_type.184
  306.4 72.6 %all-reduce.14.cloned.1.call-done = (bf16[768,1024]{1,0:T(8,128)(2,1)}, bf16[768,1024]{1,0:T(8,128)(2,1)}) async-done(((bf16[768,1024]{1,0:T(8,128)(2,1)}, bf16[768,1024]{1,0:T(8,128)(2,1)}), (bf16[768,1024]{1,0:T(8,128)(2,1)}, bf16[768,1024]{1,0:T(8,128)(2,1)})) %all-reduce.14.cloned.1.call-update) | async-done | bytes 3145744 | tf_op jit(solution)/shard_map/psum | solution.py:256
  379.0 1.9 convert_element_type.194
  382.3 1.9 dynamic-slice_reduce_fusion.1
  384.3 65.2 %all-reduce = (f32[1024]{0:T(1024)}, f32[1024]{0:T(1024)}, f32[1024]{0:T(1024)}, f32[1024]{0:T(1024)}) all-reduce(f32[1024]{0:T(1024)S(1)} %get-tuple-element.57, f32[1024]{0:T(1024)S(1)} %get-tuple-element.56, f32[1024]{0:T(1024)S(1)} %get-tuple-element.55, ...), channel_id=1, replica_groups=mesh['wide'=16,'narrow'=8] {'wide','narrow'}, use_global_device_ids=true, to_apply=%region_24.25 | all-reduce | flops 4096 | bytes 32768 | tf_op jit(solution)/shard_map/psum | solution.py:303
  449.5 1.8 dynamic-slice_add_fusion.1
  451.3 81.8 %all-reduce.12.cloned.1.call-done = (bf16[1024,128]{1,0:T(8,128)(2,1)}, bf16[1024,128]{1,0:T(8,128)(2,1)}, bf16[128,1024]{1,0:T(8,128)(2,1)}, bf16[1024,512]{1,0...) async-done(((bf16[1024,128]{1,0:T(8,128)(2,1)}, bf16[1024,128]{1,0:T(8,128)(2,1)}, bf16[128,1024]{1,0:T(8,128)(2,1)}, bf16[1024,512]{1,0:T(8,128)(2,1)}, ...) | async-done | bytes 3932176 | tf_op jit(solution)/shard_map/psum | solution.py:296
  533.1 1.9 convert_element_type.198
  535.0 1.8 convert_element_type.200
  536.8 1.8 convert_element_type.202
  538.6 2.9 convert_element_type.204
  544.7 48.3 %all-gather.9.cloned.1.call-done = bf16[16384,128]{1,0:T(8,128)(2,1)} async-done(((bf16[1024,128]{1,0:T(8,128)(2,1)}), bf16[16384,128]{1,0:T(8,128)(2,1)}) %all-gather.9.cloned.1.call-update) | async-done | bytes 4194320 | tf_op jit(solution)/shard_map/all_gather | solution.py:293
  593.0 2.9 reduce_sum.150
  (165 shorter events, 36.0 us)
Async XLA Ops:
  7.2 178.8 %copy-start = (bf16[512,1024]{1,0:T(8,128)(2,1)S(1)}, bf16[512,1024]{1,0:T(8,128)(2,1)}, u32[]{:S(2)}) copy-start(bf16[512,1024]{1,0:T(8,128)(2,1)} %param.23) | copy-start | bytes 3145732
  7.2 49.4 %copy-start.45 = (f32[1024]{0:T(1024)S(1)}, f32[1024]{0:T(1024)}, u32[]{:S(2)}) copy-start(f32[1024]{0:T(1024)} %param.24) | copy-start | bytes 12292
  7.2 49.4 %copy-start.46 = (f32[1024]{0:T(1024)S(1)}, f32[1024]{0:T(1024)}, u32[]{:S(2)}) copy-start(f32[1024]{0:T(1024)} %param.25) | copy-start | bytes 12292
  7.2 45.6 %all-gather.5.cloned.1.call-start = ((), (), s32[]{:S(2)}) async-start(), calls=%async_computation | async-start | bytes 1769472 | tf_op jit(solution)/shard_map/all_gather | solution.py:241
  8.0 136.2 %all-reduce.8.cloned.1.call-start = ((), (), s32[]{:S(2)}) async-start(), calls=%async_computation.1 | async-start | bytes 3145728 | tf_op jit(solution)/shard_map/psum | solution.py:250
  11.5 45.8 %copy-start.24 = (bf16[1024,128]{1,0:T(8,128)(2,1)S(1)}, bf16[1024,128]{1,0:T(8,128)(2,1)}, u32[]{:S(2)}) copy-start(bf16[1024,128]{1,0:T(8,128)(2,1)} %param.19) | copy-start | bytes 786436
  52.8 3.9 copy-start.2
  54.6 3.4 copy-start.21
  58.0 3.3 copy-start.33
  60.7 2.1 copy-start.5
  65.3 120.8 %all-gather.7.cloned.1.call-start = ((), (), s32[]{:S(2)}) async-start(), calls=%async_computation.2 | async-start | bytes 1769472 | tf_op jit(solution)/shard_map/all_gather | solution.py:242
  66.0 80.9 %copy-start.44 = (f32[1024]{0:T(1024)S(1)}, f32[1024]{0:T(1024)}, u32[]{:S(2)}) copy-start(f32[1024]{0:T(1024)} %param.26) | copy-start | bytes 12292
  66.0 80.9 %copy-start.47 = (f32[1024]{0:T(1024)S(1)}, f32[1024]{0:T(1024)}, u32[]{:S(2)}) copy-start(f32[1024]{0:T(1024)} %param.27) | copy-start | bytes 12292
  66.0 207.8 %all-reduce.10.cloned.1.call-start = ((), (), s32[]{:S(2)}) async-start(), calls=%async_computation.3 | async-start | bytes 3145728 | tf_op jit(solution)/shard_map/psum | solution.py:263
  146.9 3.5 copy-start.17
  150.5 2.1 copy-start.13
  150.5 2.1 copy-start.15
  186.0 5.0 copy-start.16
  195.0 184.1 %all-reduce.14.cloned.1.call-start = ((), (), s32[]{:S(2)}) async-start(), calls=%async_computation.6 | async-start | bytes 6291456 | tf_op jit(solution)/shard_map/psum | solution.py:256
  273.8 3.3 copy-start.8
  273.8 3.8 copy-start.9
  273.9 7.0 %slice-start = ((s8[4718592]{0:T(1024)(128)(4,1)}), s8[4194304]{0:T(1024)(128)(4,1)S(1)}, s32[]{:S(2)}) async-start(s8[4718592]{0:T(1024)(128)(4,1)} %bitcast.75), calls=%async_computation.7 | async-start | bytes 8388608
  277.6 3.3 slice-start.1
  288.6 3.9 copy-start.29
  288.7 244.5 %all-reduce.12.cloned.1.call-start = ((), (), s32[]{:S(2)}) async-start(), calls=%async_computation.5 | async-start | bytes 7864320 | tf_op jit(solution)/shard_map/psum | solution.py:296
  288.7 3.8 copy-start.14
  296.6 2.6 copy-start.7
  296.6 2.6 copy-start.32
  300.4 292.6 %all-gather.9.cloned.1.call-start = ((), (), s32[]{:S(2)}) async-start(), calls=%async_computation.4 | async-start | bytes 4456448 | tf_op jit(solution)/shard_map/all_gather | solution.py:293
  533.1 8.4 %copy-start.20 = (bf16[1024,512]{1,0:T(8,128)(2,1)S(1)}, bf16[1024,512]{1,0:T(8,128)(2,1)}, u32[]{:S(2)}) copy-start(bf16[1024,512]{1,0:T(8,128)(2,1)} %get-tuple-element.80) | copy-start | bytes 3145732
  538.6 4.5 copy-start.19
  543.1 53.6 %copy-start.1 = (bf16[512,1024]{1,0:T(8,128)(2,1)S(1)}, bf16[512,1024]{1,0:T(8,128)(2,1)}, u32[]{:S(2)}) copy-start(bf16[512,1024]{1,0:T(8,128)(2,1)} %param.23) | copy-start | bytes 3145732
  (26 other events, 41.7 us)
Sparse Core Ops, SparseCore 0:
  9.7 43.0 all-gather.4
  65.4 78.7 all-reduce.7
  145.8 40.1 all-gather.6
  195.1 78.7 all-reduce.9
  288.8 90.2 all-reduce.13
  382.5 150.6 all-reduce.11
  536.4 56.5 all-gather.8
